TPU v7x, 256 devices: a whole 4x4x8 slice. The times are simulated.
256 devices in a mesh: rows: 64 (over z, x, core), cols: 4 (over y).
Axes of the slice: x: 4, y: 4, z: 8, core: 2. Of those that a mesh axis runs over, the one named last changes fastest.
Arguments:
- pass_rates: float32 [32, 1048576], P(None, 'rows'), may hold values from 0 to 1
- upper_blocks: bfloat16 [8192, 8, 128, 128], P('rows', 'cols'), may hold values from 9.9658966e-05 to 0.0099487305
- neighbours: int32 [8192, 8], P('rows', 'cols'), may hold values from 0 to 8191, as said below
Outputs:
- solution: float32 [32, 1048576], P('cols', 'rows')
- residual: float32 [32, 1048576], P('cols', 'rows')
Inputs may be any that keep to these rules, and one draw needn't show every extreme that they name: `neighbours`: slot 0 of block-row b names b itself; every other slot of block-row b names a block from b to b + 256 that exists; in the last block-row of every shard of 128 block-rows, slot 1 names the farthest such block.
All inputs are finite; a program needn't handle non-finite values.
Results may differ from a plain program's by a relative error of at most 0.034.
Values may be sent and summed in bfloat16 or wider, within the bound.
A program may use at most 128 MiB of HBM per device.

v0:
```python
import jax
import jax.numpy as jnp
from jax import lax
from jax.sharding import PartitionSpec as P

REACH = 2
ITERS = 2


def from_behind(value, axis, steps):
    count = lax.axis_size(axis)
    initial, last = (max(0, -steps), min(count, count - steps))
    return lax.ppermute(value, axis, [(source, source + steps) for source in range(initial, last)])


def per_device(pass_rates, upper_blocks, neighbours):
    shard_rows = upper_blocks.shape[0]
    block_width = upper_blocks.shape[2]
    columns = pass_rates.shape[0]
    first_block = lax.axis_index("rows") * shard_rows
    local_index = neighbours - first_block
    own_weight = jnp.sum(upper_blocks, axis=(1, 3), dtype=jnp.float32)
    col_weight = jnp.sum(upper_blocks, axis=2, dtype=jnp.float32)
    share = columns // lax.axis_size("cols")
    residual = pass_rates

    def squares(values):
        return lax.psum(jnp.sum(values * values, axis=1), "rows")

    solution = jnp.zeros_like(residual)
    direction = residual
    norm_now = squares(residual)
    for iteration in range(ITERS):
        rounded = direction.astype(jnp.bfloat16)
        pieces = [rounded]
        for distance in range(1, REACH + 1):
            pieces.append(from_behind(rounded, "rows", -distance))
        window = jnp.concatenate(pieces, axis=1).reshape(
            columns, (REACH + 1) * shard_rows, block_width
        )
        own_block = rounded.reshape(columns, shard_rows, block_width)
        far_blocks = jnp.take(window, local_index, axis=1)
        forward = own_block.astype(jnp.float32) * own_weight[None] - jnp.einsum(
            "bkij,cbkj->cbi", upper_blocks, far_blocks, preferred_element_type=jnp.float32
        )
        transposed = col_weight[None] * far_blocks.astype(jnp.float32) - jnp.einsum(
            "bkij,cbi->cbkj", upper_blocks, own_block, preferred_element_type=jnp.float32
        )
        returned = jnp.zeros(window.shape, jnp.float32).at[:, local_index].add(transposed)
        summed = forward + returned[:, :shard_rows]
        for distance in range(1, REACH + 1):
            summed = summed + from_behind(
                returned[:, distance * shard_rows : (distance + 1) * shard_rows], "rows", distance
            )
        spread = lax.psum(summed, "cols")
        mapped = direction + 0.5 * spread.reshape(direction.shape)
        step_size = norm_now / lax.psum(jnp.sum(direction * mapped, axis=1), "rows")
        solution = solution + step_size[:, None] * direction
        residual = residual - step_size[:, None] * mapped
        if iteration + 1 < ITERS:
            norm_next = squares(residual)
            direction = residual + (norm_next / norm_now)[:, None] * direction
            norm_now = norm_next
    solution = lax.dynamic_slice_in_dim(solution, lax.axis_index("cols") * share, share, 0)
    residual = lax.dynamic_slice_in_dim(residual, lax.axis_index("cols") * share, share, 0)
    return (solution, residual)


def solution(mesh):
    in_specs = (P(None, "rows"), P("rows", "cols", None, None), P("rows", "cols"))
    out_specs = (P("cols", "rows"), P("cols", "rows"))
    return jax.shard_map(
        per_device, mesh=mesh, in_specs=in_specs, out_specs=out_specs, check_vma=False
    )
```

profile of v0, /device:TPU:8, one launch (start us, length us, event | category | flops | bytes accessed | tf_op | source)
XLA Modules:
  0.0 888.1 jit_solution(16670303994397478807)
XLA Ops:
  7.2 2.8 convert_element_type.22
  10.0 1.3 collective-permute-start.1
  11.3 1.3 collective-permute-start
  12.7 0.1 copy.19
  12.8 0.1 copy.20
  12.9 0.1 reshape.76
  13.1 0.1 convert_bitcast_fusion.1
  13.2 0.2 copy.45
  13.5 5.8 convert_reduce_fusion.1
  19.3 17.8 %collective-permute-done.1 = bf16[32,16384]{1,0:T(8,128)(2,1)} collective-permute-done((bf16[32,16384]{1,0:T(8,128)(2,1)}, bf16[32,16384]{1,0:T(8,128)(2,1)}, u32[]{:S(2)}, u32[]{:S(2)}) %collective-permute-start.1) | collective-permute-done | bytes 1048608 | tf_op jit(solution)/shard_map/ppermute | solution.py:13
  37.1 3.3 copy_bitcast_fusion.1
  40.4 4.0 gather_fusion
  44.5 8.5 bitcast_subtract_fusion.1
  53.0 3.5 broadcast.23.clone
  56.4 34.0 %scatter_fusion = f32[32,384,128]{2,0,1:T(8,128)} fusion(f32[32,384,128]{2,0,1:T(8,128)} %broadcast.23.clone, s32[256]{0:T(256)S(1)} %reshape.76, f32[256,32,128]{2,1,0:T(8,128)} %bitcast.94), kind=kCustom, calls=%fused_computation.2 | custom fusion | flops 1048576 | bytes 12583936 | tf_op jit(solution)/shard_map/scatter-add | solution.py:49
  90.4 2.8 fusion.21
  93.2 13.1 %collective-permute-start.2 = (f32[32,128,128]{2,0,1:T(8,128)S(1)}, f32[32,128,128]{2,0,1:T(8,128)S(1)}, u32[]{:S(2)}, u32[]{:S(2)}) collective-permute-start(f32[32,128,128]{2,0,1:T(8,128)S(1)} %get-tuple-element.17), channel_id=1, source_target_pairs={{0,4},{4,8},{8,12},{12,16},{16,20},{20,24},{24,28},{28,32},{32,36}... | collective-permute-start | bytes 6291464 | tf_op jit(solution)/shard_map/ppermute | solution.py:13
  106.3 3.4 collective-permute-start.3
  109.7 0.2 collective-permute-done.2
  109.9 45.7 %collective-permute-done.3 = f32[32,128,128]{2,0,1:T(8,128)S(1)} collective-permute-done((f32[32,128,128]{2,0,1:T(8,128)S(1)}, f32[32,128,128]{2,0,1:T(8,128)S(1)}, u32[]{:S(2)}, u32[]{:S(2)}) %collective-permute-start.3) | collective-permute-done | bytes 2097184 | tf_op jit(solution)/shard_map/ppermute | solution.py:13
  155.7 8.3 fusion.3
  164.0 87.0 %all-reduce.4.cloned.1.call-done = f32[32,128,128]{2,0,1:T(8,128)} async-done(((f32[32,128,128]{2,0,1:T(8,128)}), f32[32,128,128]{2,0,1:T(8,128)}) %all-reduce.4.cloned.1.call-update) | async-done | bytes 2097168 | tf_op jit(solution)/shard_map/psum | solution.py:55
  251.1 2.1 multiply_reduce_fusion.2
  253.2 128.9 %all-reduce = (f32[32]{0:T(128)S(1)}, f32[32]{0:T(128)S(1)}) all-reduce(f32[32]{0:T(128)S(1)} %get-tuple-element.6, f32[32]{0:T(128)S(1)} %get-tuple-element.5), channel_id=1, replica_groups=mesh['rows'=64,'cols'=4] {'rows'}, use_global_device_ids=true, to_apply=%region_1.0 | all-reduce | flops 64 | bytes 512 | tf_op jit(solution)/shard_map/psum | solution.py:28
  382.1 3.4 multiply_reduce_fusion.1
  385.5 124.1 %psum.45 = f32[32]{0:T(128)S(1)} all-reduce(f32[32]{0:T(128)S(1)} %get-tuple-element.11), channel_id=1, replica_groups=mesh['rows'=64,'cols'=4] {'rows'}, use_global_device_ids=true, to_apply=%region_9.11 | all-reduce | flops 32 | bytes 256 | tf_op jit(solution)/shard_map/psum | solution.py:28
  509.6 3.3 fusion.19
  512.9 1.3 collective-permute-start.5
  514.2 1.5 collective-permute-start.4
  515.6 1.2 copy.46
  516.8 22.8 %collective-permute-done.5 = bf16[32,16384]{1,0:T(8,128)(2,1)S(1)} collective-permute-done((bf16[32,16384]{1,0:T(8,128)(2,1)S(1)}, bf16[32,16384]{1,0:T(8,128)(2,1)S(1)}, u32[]{:S(2)}, u32[]{:S(2)}) %collective-permute-start.5) | collective-permute-done | bytes 1048608 | tf_op jit(solution)/shard_map/ppermute | solution.py:13
  539.7 1.9 copy_bitcast_fusion
  541.6 4.1 gather_fusion.1
  545.7 8.7 bitcast_subtract_fusion
  554.4 3.5 broadcast.23
  557.8 34.0 %scatter_fusion.1 = f32[32,384,128]{2,0,1:T(8,128)} fusion(f32[32,384,128]{2,0,1:T(8,128)} %broadcast.23, s32[256]{0:T(256)S(1)} %reshape.76, f32[256,32,128]{2,1,0:T(8,128)} %bitcast.93), kind=kCustom, calls=%fused_computation.3 | custom fusion | flops 1048576 | bytes 12583936 | tf_op jit(solution)/shard_map/scatter-add | solution.py:49
  591.8 2.8 fusion.20
  594.6 13.1 %collective-permute-start.6 = (f32[32,128,128]{2,0,1:T(8,128)S(1)}, f32[32,128,128]{2,0,1:T(8,128)S(1)}, u32[]{:S(2)}, u32[]{:S(2)}) collective-permute-start(f32[32,128,128]{2,0,1:T(8,128)S(1)} %get-tuple-element.15), channel_id=1, source_target_pairs={{0,4},{4,8},{8,12},{12,16},{16,20},{20,24},{24,28},{28,32},{32,36}... | collective-permute-start | bytes 6291464 | tf_op jit(solution)/shard_map/ppermute | solution.py:13
  607.7 1.7 collective-permute-start.7
  609.3 2.0 collective-permute-done.6
  611.3 44.0 %collective-permute-done.7 = f32[32,128,128]{2,0,1:T(8,128)S(1)} collective-permute-done((f32[32,128,128]{2,0,1:T(8,128)S(1)}, f32[32,128,128]{2,0,1:T(8,128)S(1)}, u32[]{:S(2)}, u32[]{:S(2)}) %collective-permute-start.7) | collective-permute-done | bytes 2097184 | tf_op jit(solution)/shard_map/ppermute | solution.py:13
  655.3 8.3 fusion.1
  663.6 0.1 dynamic-slice
  663.7 82.1 %all-reduce.6.cloned.1.call-done = f32[32,128,128]{2,0,1:T(8,128)} async-done(((f32[32,128,128]{2,0,1:T(8,128)}), f32[32,128,128]{2,0,1:T(8,128)}) %all-reduce.6.cloned.1.call-update) | async-done | bytes 2097168 | tf_op jit(solution)/shard_map/psum | solution.py:55
  745.8 4.0 bitcast_add_fusion
  749.7 128.9 %psum.47 = f32[32]{0:T(128)S(1)} all-reduce(f32[32]{0:T(128)S(1)} %get-tuple-element.20), channel_id=1, replica_groups=mesh['rows'=64,'cols'=4] {'rows'}, use_global_device_ids=true, to_apply=%region_13.15 | all-reduce | flops 32 | bytes 256 | tf_op jit(solution)/shard_map/psum | solution.py:57
  878.7 0.1 dynamic-slice.1
  878.8 2.5 dynamic-slice_subtract_fusion
  (19 shorter events, 0.2 us)
Async XLA Ops:
  7.2 5.9 copy-start
  7.2 5.5 copy-start.3
  7.2 243.9 %all-reduce.4.cloned.1.call-start = ((), (), s32[]{:S(2)}) async-start(), calls=%async_computation | async-start | bytes 4194304 | tf_op jit(solution)/shard_map/psum | solution.py:55
  10.0 27.1 %collective-permute-start.1 = (bf16[32,16384]{1,0:T(8,128)(2,1)}, bf16[32,16384]{1,0:T(8,128)(2,1)}, u32[]{:S(2)}, u32[]{:S(2)}) collective-permute-start(bf16[32,16384]{1,0:T(8,128)(2,1)} %convert_element_type.22), channel_id=1, source_target_pairs={{8,0},{12,4},{16,8},{20,12},{24,16},{28,20},{32,24},{36,28},{40,32... | collective-permute-start | bytes 3145736 | tf_op jit(solution)/shard_map/ppermute | solution.py:13
  11.3 25.8 %collective-permute-start = (bf16[32,16384]{1,0:T(8,128)(2,1)}, bf16[32,16384]{1,0:T(8,128)(2,1)}, u32[]{:S(2)}, u32[]{:S(2)}) collective-permute-start(bf16[32,16384]{1,0:T(8,128)(2,1)} %convert_element_type.22), channel_id=1, source_target_pairs={{4,0},{8,4},{12,8},{16,12},{20,16},{24,20},{28,24},{32,28},{36,32}... | collective-permute-start | bytes 3145736 | tf_op jit(solution)/shard_map/ppermute | solution.py:13
  90.4 65.3 %copy-start.1 = (bf16[256,32,128]{2,1,0:T(8,128)(2,1)S(1)}, bf16[256,32,128]{2,1,0:T(8,128)(2,1)}, u32[]{:S(2)}) copy-start(bf16[256,32,128]{2,1,0:T(8,128)(2,1)} %gather_fusion) | copy-start | bytes 6291460
  93.2 16.7 %collective-permute-start.2 = (f32[32,128,128]{2,0,1:T(8,128)S(1)}, f32[32,128,128]{2,0,1:T(8,128)S(1)}, u32[]{:S(2)}, u32[]{:S(2)}) collective-permute-start(f32[32,128,128]{2,0,1:T(8,128)S(1)} %get-tuple-element.17), channel_id=1, source_target_pairs={{0,4},{4,8},{8,12},{12,16},{16,20},{20,24},{24,28},{28,32},{32,36}... | collective-permute-start | bytes 6291464 | tf_op jit(solution)/shard_map/ppermute | solution.py:13
  106.3 49.4 %collective-permute-start.3 = (f32[32,128,128]{2,0,1:T(8,128)S(1)}, f32[32,128,128]{2,0,1:T(8,128)S(1)}, u32[]{:S(2)}, u32[]{:S(2)}) collective-permute-start(f32[32,128,128]{2,0,1:T(8,128)S(1)} %get-tuple-element.18), channel_id=1, source_target_pairs={{0,8},{4,12},{8,16},{12,20},{16,24},{20,28},{24,32},{28,36},{32,40... | collective-permute-start | bytes 6291464 | tf_op jit(solution)/shard_map/ppermute | solution.py:13
  164.0 581.8 %all-reduce.6.cloned.1.call-start = ((), (), s32[]{:S(2)}) async-start(), calls=%async_computation.1 | async-start | bytes 4194304 | tf_op jit(solution)/shard_map/psum | solution.py:55
  512.9 26.8 %collective-permute-start.5 = (bf16[32,16384]{1,0:T(8,128)(2,1)S(1)}, bf16[32,16384]{1,0:T(8,128)(2,1)S(1)}, u32[]{:S(2)}, u32[]{:S(2)}) collective-permute-start(bf16[32,16384]{1,0:T(8,128)(2,1)S(1)} %get-tuple-element.9), channel_id=1, source_target_pairs={{8,0},{12,4},{16,8},{20,12},{24,16},{28,20},{32,24},{36,28},{40,32... | collective-permute-start | bytes 3145736 | tf_op jit(solution)/shard_map/ppermute | solution.py:13
  514.2 25.5 %collective-permute-start.4 = (bf16[32,16384]{1,0:T(8,128)(2,1)S(1)}, bf16[32,16384]{1,0:T(8,128)(2,1)S(1)}, u32[]{:S(2)}, u32[]{:S(2)}) collective-permute-start(bf16[32,16384]{1,0:T(8,128)(2,1)S(1)} %get-tuple-element.9), channel_id=1, source_target_pairs={{4,0},{8,4},{12,8},{16,12},{20,16},{24,20},{28,24},{32,28},{36,32}... | collective-permute-start | bytes 3145736 | tf_op jit(solution)/shard_map/ppermute | solution.py:13
  591.8 63.5 %copy-start.2 = (bf16[256,32,128]{2,1,0:T(8,128)(2,1)S(1)}, bf16[256,32,128]{2,1,0:T(8,128)(2,1)}, u32[]{:S(2)}) copy-start(bf16[256,32,128]{2,1,0:T(8,128)(2,1)} %gather_fusion.1) | copy-start | bytes 6291460
  594.6 16.7 %collective-permute-start.6 = (f32[32,128,128]{2,0,1:T(8,128)S(1)}, f32[32,128,128]{2,0,1:T(8,128)S(1)}, u32[]{:S(2)}, u32[]{:S(2)}) collective-permute-start(f32[32,128,128]{2,0,1:T(8,128)S(1)} %get-tuple-element.15), channel_id=1, source_target_pairs={{0,4},{4,8},{8,12},{12,16},{16,20},{20,24},{24,28},{28,32},{32,36}... | collective-permute-start | bytes 6291464 | tf_op jit(solution)/shard_map/ppermute | solution.py:13
  607.7 47.6 %collective-permute-start.7 = (f32[32,128,128]{2,0,1:T(8,128)S(1)}, f32[32,128,128]{2,0,1:T(8,128)S(1)}, u32[]{:S(2)}, u32[]{:S(2)}) collective-permute-start(f32[32,128,128]{2,0,1:T(8,128)S(1)} %get-tuple-element.16), channel_id=1, source_target_pairs={{0,8},{4,12},{8,16},{12,20},{16,24},{20,28},{24,32},{28,36},{32,40... | collective-permute-start | bytes 6291464 | tf_op jit(solution)/shard_map/ppermute | solution.py:13
Sparse Core Ops, SparseCore 0:
  164.1 86.9 all-reduce.3
  663.8 81.9 all-reduce.5
where the time goes:
time: 889 us; the launch traced here: 888 us
  blocking collectives  382 us (43%)
  waiting for transfers between devices  302 us (34%)
  other arithmetic  97.2 us (11%)
  starting transfers between devices  36.6 us (4%)
  matrix products  33.8 us (4%)
  local copies, waits for them, and re-layouts  22.7 us (3%)
  between operations  14.2 us (2%)
    psum x2, blocking collectives, squares(): return lax.psum(jnp.sum(values * values, axis=1), 'rows')  253 us
    psum x2, waiting for transfers between devices, per_device(): spread = lax.psum(summed, 'cols')  169 us
    ppermute x8, waiting for transfers between devices, from_behind(): lax.ppermute(value, axis, [(source, source + steps) for source in range(i...  133 us
    psum x1, blocking collectives, per_device(): step_size = norm_now / lax.psum(jnp.sum(direction * mapped, axis=1), 'rows')  129 us
    scatter-add x2, other arithmetic, per_device(): jnp.zeros(window.shape, jnp.float32).at[:, local_index].add(transposed)  67.9 us
    ppermute x8, starting transfers between devices, from_behind(): lax.ppermute(value, axis, [(source, source + steps) for source in range(i...  36.5 us
  transfers between devices with their start and end apart: 10, of which 8 were waited for; matrix products, arithmetic and copies ran while one was open for 1% of the time, Pallas kernels for 0%

commit v1 on v0

--- a/solution.py
+++ b/solution.py
@@ -52,7 +52,7 @@
             summed = summed + from_behind(
                 returned[:, distance * shard_rows : (distance + 1) * shard_rows], "rows", distance
             )
-        spread = lax.psum(summed, "cols")
+        spread = jnp.sum(lax.all_gather(summed, "cols"), axis=0)
         mapped = direction + 0.5 * spread.reshape(direction.shape)
         step_size = norm_now / lax.psum(jnp.sum(direction * mapped, axis=1), "rows")
         solution = solution + step_size[:, None] * direction

time: 889 us -> 949 us (1.067)
  waiting for transfers between devices: 302 us -> 350 us
  other arithmetic: 97.2 us -> 110 us
    all_gather x0 -> x2, waiting for transfers between devices: none -> 223 us  [per_device(): spread = jnp.sum(lax.all_gather(summed, 'cols'), axis=0)]
    psum x2 -> x0, waiting for transfers between devices: 169 us -> none  [per_device(): spread = lax.psum(summed, 'cols')]
    reduce_sum x0 -> x2, other arithmetic: none -> 12.3 us  [per_device(): spread = jnp.sum(lax.all_gather(summed, 'cols'), axis=0)]
  transfers between devices with their start and end apart: 10 -> 10, of which waited for: 8 -> 6; matrix products, arithmetic and copies ran while one was open for 1% -> 1% of each run, Pallas kernels for 0% -> 0%
where the time goes in v1:
time: 949 us; the launch traced here: 948 us
  blocking collectives  382 us (40%)
  waiting for transfers between devices  350 us (37%)
  other arithmetic  110 us (12%)
  starting transfers between devices  36.2 us (4%)
  matrix products  33.9 us (4%)
  local copies, waits for them, and re-layouts  22.7 us (2%)
  between operations  14.2 us (1%)
    psum x2, blocking collectives, squares(): return lax.psum(jnp.sum(values * values, axis=1), 'rows')  253 us
    all_gather x2, waiting for transfers between devices, per_device(): spread = jnp.sum(lax.all_gather(summed, 'cols'), axis=0)  223 us
    psum x1, blocking collectives, per_device(): step_size = norm_now / lax.psum(jnp.sum(direction * mapped, axis=1), 'rows')  129 us
    ppermute x8, waiting for transfers between devices, from_behind(): lax.ppermute(value, axis, [(source, source + steps) for source in range(i...  127 us
    scatter-add x2, other arithmetic, per_device(): jnp.zeros(window.shape, jnp.float32).at[:, local_index].add(transposed)  67.9 us
    ppermute x8, starting transfers between devices, from_behind(): lax.ppermute(value, axis, [(source, source + steps) for source in range(i...  36 us
  transfers between devices with their start and end apart: 10, of which 6 were waited for; matrix products, arithmetic and copies ran while one was open for 1% of the time, Pallas kernels for 0%

profile of v1, /device:TPU:8, one launch (start us, length us, event | category | flops | bytes accessed | tf_op | source)
XLA Modules:
  0.0 947.9 jit_solution(2310999546415678535)
XLA Ops:
  7.2 2.8 convert_element_type.22
  10.0 1.3 collective-permute-start.1
  11.3 1.3 collective-permute-start
  12.7 0.1 copy.40
  12.8 0.1 reshape.78
  12.9 0.1 copy.39
  13.1 0.1 convert_bitcast_fusion.1
  13.2 0.2 copy.65
  13.5 5.8 convert_reduce_fusion.1
  19.3 17.8 %collective-permute-done.1 = bf16[32,16384]{1,0:T(8,128)(2,1)} collective-permute-done((bf16[32,16384]{1,0:T(8,128)(2,1)}, bf16[32,16384]{1,0:T(8,128)(2,1)}, u32[]{:S(2)}, u32[]{:S(2)}) %collective-permute-start.1) | collective-permute-done | bytes 1048608 | tf_op jit(solution)/shard_map/ppermute | solution.py:13
  37.1 3.3 copy_bitcast_fusion.1
  40.4 4.0 gather_fusion
  44.5 8.5 bitcast_subtract_fusion.1
  53.0 3.5 broadcast.23.clone
  56.4 34.0 %scatter_fusion = f32[32,384,128]{2,0,1:T(8,128)} fusion(f32[32,384,128]{2,0,1:T(8,128)} %broadcast.23.clone, s32[256]{0:T(256)S(1)} %reshape.78, f32[256,32,128]{2,1,0:T(8,128)} %bitcast.96), kind=kCustom, calls=%fused_computation.2 | custom fusion | flops 1048576 | bytes 12583936 | tf_op jit(solution)/shard_map/scatter-add | solution.py:49
  90.4 2.8 fusion.21
  93.2 12.8 %collective-permute-start.3 = (f32[32,128,128]{2,0,1:T(8,128)S(1)}, f32[32,128,128]{2,0,1:T(8,128)S(1)}, u32[]{:S(2)}, u32[]{:S(2)}) collective-permute-start(f32[32,128,128]{2,0,1:T(8,128)S(1)} %get-tuple-element.18), channel_id=1, source_target_pairs={{0,8},{4,12},{8,16},{12,20},{16,24},{20,28},{24,32},{28,36},{32,40... | collective-permute-start | bytes 6291464 | tf_op jit(solution)/shard_map/ppermute | solution.py:13
  106.0 3.5 collective-permute-start.2
  109.6 41.6 %collective-permute-done.3 = f32[32,128,128]{2,0,1:T(8,128)S(1)} collective-permute-done((f32[32,128,128]{2,0,1:T(8,128)S(1)}, f32[32,128,128]{2,0,1:T(8,128)S(1)}, u32[]{:S(2)}, u32[]{:S(2)}) %collective-permute-start.3) | collective-permute-done | bytes 2097184 | tf_op jit(solution)/shard_map/ppermute | solution.py:13
  151.2 8.3 fusion.3
  159.5 0.2 all-gather.7.cloned.1.call-start
  159.7 114.9 %all-gather.5.cloned.1.call-done = f32[128,128,128]{2,0,1:T(8,128)} async-done(((f32[32,128,128]{2,0,1:T(8,128)}), f32[128,128,128]{2,0,1:T(8,128)}) %all-gather.5.cloned.1.call-update) | async-done | bytes 8388624 | tf_op jit(solution)/shard_map/all_gather | solution.py:55
  274.7 6.2 reduce_sum.75
  280.8 2.1 multiply_reduce_fusion.2
  282.9 128.9 %all-reduce = (f32[32]{0:T(128)S(1)}, f32[32]{0:T(128)S(1)}) all-reduce(f32[32]{0:T(128)S(1)} %get-tuple-element.6, f32[32]{0:T(128)S(1)} %get-tuple-element.5), channel_id=1, replica_groups=mesh['rows'=64,'cols'=4] {'rows'}, use_global_device_ids=true, to_apply=%region_1.0 | all-reduce | flops 64 | bytes 512 | tf_op jit(solution)/shard_map/psum | solution.py:28
  411.8 3.4 multiply_reduce_fusion.1
  415.3 124.1 %psum.30 = f32[32]{0:T(128)S(1)} all-reduce(f32[32]{0:T(128)S(1)} %get-tuple-element.11), channel_id=1, replica_groups=mesh['rows'=64,'cols'=4] {'rows'}, use_global_device_ids=true, to_apply=%region_9.11 | all-reduce | flops 32 | bytes 256 | tf_op jit(solution)/shard_map/psum | solution.py:28
  539.3 3.3 fusion.19
  542.6 1.3 collective-permute-start.5
  543.9 1.3 collective-permute-start.4
  545.2 1.2 copy.66
  546.4 23.0 %collective-permute-done.5 = bf16[32,16384]{1,0:T(8,128)(2,1)S(1)} collective-permute-done((bf16[32,16384]{1,0:T(8,128)(2,1)S(1)}, bf16[32,16384]{1,0:T(8,128)(2,1)S(1)}, u32[]{:S(2)}, u32[]{:S(2)}) %collective-permute-start.5) | collective-permute-done | bytes 1048608 | tf_op jit(solution)/shard_map/ppermute | solution.py:13
  569.4 1.9 copy_bitcast_fusion
  571.3 4.1 gather_fusion.1
  575.4 8.7 bitcast_subtract_fusion
  584.1 3.5 broadcast.23
  587.5 34.0 %scatter_fusion.1 = f32[32,384,128]{2,0,1:T(8,128)} fusion(f32[32,384,128]{2,0,1:T(8,128)} %broadcast.23, s32[256]{0:T(256)S(1)} %reshape.78, f32[256,32,128]{2,1,0:T(8,128)} %bitcast.95), kind=kCustom, calls=%fused_computation.3 | custom fusion | flops 1048576 | bytes 12583936 | tf_op jit(solution)/shard_map/scatter-add | solution.py:49
  621.5 2.8 fusion.20
  624.3 12.8 %collective-permute-start.7 = (f32[32,128,128]{2,0,1:T(8,128)S(1)}, f32[32,128,128]{2,0,1:T(8,128)S(1)}, u32[]{:S(2)}, u32[]{:S(2)}) collective-permute-start(f32[32,128,128]{2,0,1:T(8,128)S(1)} %get-tuple-element.16), channel_id=1, source_target_pairs={{0,8},{4,12},{8,16},{12,20},{16,24},{20,28},{24,32},{28,36},{32,40... | collective-permute-start | bytes 6291464 | tf_op jit(solution)/shard_map/ppermute | solution.py:13
  637.1 1.7 collective-permute-start.6
  638.8 44.2 %collective-permute-done.7 = f32[32,128,128]{2,0,1:T(8,128)S(1)} collective-permute-done((f32[32,128,128]{2,0,1:T(8,128)S(1)}, f32[32,128,128]{2,0,1:T(8,128)S(1)}, u32[]{:S(2)}, u32[]{:S(2)}) %collective-permute-start.7) | collective-permute-done | bytes 2097184 | tf_op jit(solution)/shard_map/ppermute | solution.py:13
  683.0 8.4 fusion.1
  691.5 108.0 %all-gather.7.cloned.1.call-done = f32[128,128,128]{2,0,1:T(8,128)} async-done(((f32[32,128,128]{2,0,1:T(8,128)}), f32[128,128,128]{2,0,1:T(8,128)}) %all-gather.7.cloned.1.call-update) | async-done | bytes 8388624 | tf_op jit(solution)/shard_map/all_gather | solution.py:55
  799.5 6.2 reduce_sum.78
  805.7 4.0 bitcast_add_fusion
  809.6 128.9 %psum.31 = f32[32]{0:T(128)S(1)} all-reduce(f32[32]{0:T(128)S(1)} %get-tuple-element.20), channel_id=1, replica_groups=mesh['rows'=64,'cols'=4] {'rows'}, use_global_device_ids=true, to_apply=%region_13.15 | all-reduce | flops 32 | bytes 256 | tf_op jit(solution)/shard_map/psum | solution.py:57
  938.5 0.1 dynamic-slice.1
  938.6 2.5 dynamic-slice_subtract_fusion
  (21 shorter events, 0.2 us)
Async XLA Ops:
  7.2 5.9 copy-start
  7.2 5.5 copy-start.3
  7.2 267.5 %all-gather.5.cloned.1.call-start = ((), (), s32[]{:S(2)}) async-start(), calls=%async_computation | async-start | bytes 10485760 | tf_op jit(solution)/shard_map/all_gather | solution.py:55
  10.0 27.1 %collective-permute-start.1 = (bf16[32,16384]{1,0:T(8,128)(2,1)}, bf16[32,16384]{1,0:T(8,128)(2,1)}, u32[]{:S(2)}, u32[]{:S(2)}) collective-permute-start(bf16[32,16384]{1,0:T(8,128)(2,1)} %convert_element_type.22), channel_id=1, source_target_pairs={{8,0},{12,4},{16,8},{20,12},{24,16},{28,20},{32,24},{36,28},{40,32... | collective-permute-start | bytes 3145736 | tf_op jit(solution)/shard_map/ppermute | solution.py:13
  11.3 25.8 %collective-permute-start = (bf16[32,16384]{1,0:T(8,128)(2,1)}, bf16[32,16384]{1,0:T(8,128)(2,1)}, u32[]{:S(2)}, u32[]{:S(2)}) collective-permute-start(bf16[32,16384]{1,0:T(8,128)(2,1)} %convert_element_type.22), channel_id=1, source_target_pairs={{4,0},{8,4},{12,8},{16,12},{20,16},{24,20},{28,24},{32,28},{36,32}... | collective-permute-start | bytes 3145736 | tf_op jit(solution)/shard_map/ppermute | solution.py:13
  90.4 60.7 %copy-start.1 = (bf16[256,32,128]{2,1,0:T(8,128)(2,1)S(1)}, bf16[256,32,128]{2,1,0:T(8,128)(2,1)}, u32[]{:S(2)}) copy-start(bf16[256,32,128]{2,1,0:T(8,128)(2,1)} %gather_fusion) | copy-start | bytes 6291460
  93.2 57.9 %collective-permute-start.3 = (f32[32,128,128]{2,0,1:T(8,128)S(1)}, f32[32,128,128]{2,0,1:T(8,128)S(1)}, u32[]{:S(2)}, u32[]{:S(2)}) collective-permute-start(f32[32,128,128]{2,0,1:T(8,128)S(1)} %get-tuple-element.18), channel_id=1, source_target_pairs={{0,8},{4,12},{8,16},{12,20},{16,24},{20,28},{24,32},{28,36},{32,40... | collective-permute-start | bytes 6291464 | tf_op jit(solution)/shard_map/ppermute | solution.py:13
  106.0 45.1 %collective-permute-start.2 = (f32[32,128,128]{2,0,1:T(8,128)S(1)}, f32[32,128,128]{2,0,1:T(8,128)S(1)}, u32[]{:S(2)}, u32[]{:S(2)}) collective-permute-start(f32[32,128,128]{2,0,1:T(8,128)S(1)} %get-tuple-element.17), channel_id=1, source_target_pairs={{0,4},{4,8},{8,12},{12,16},{16,20},{20,24},{24,28},{28,32},{32,36}... | collective-permute-start | bytes 6291464 | tf_op jit(solution)/shard_map/ppermute | solution.py:13
  159.5 640.0 %all-gather.7.cloned.1.call-start = ((), (), s32[]{:S(2)}) async-start(), calls=%async_computation.1 | async-start | bytes 10485760 | tf_op jit(solution)/shard_map/all_gather | solution.py:55
  542.6 26.8 %collective-permute-start.5 = (bf16[32,16384]{1,0:T(8,128)(2,1)S(1)}, bf16[32,16384]{1,0:T(8,128)(2,1)S(1)}, u32[]{:S(2)}, u32[]{:S(2)}) collective-permute-start(bf16[32,16384]{1,0:T(8,128)(2,1)S(1)} %get-tuple-element.9), channel_id=1, source_target_pairs={{8,0},{12,4},{16,8},{20,12},{24,16},{28,20},{32,24},{36,28},{40,32... | collective-permute-start | bytes 3145736 | tf_op jit(solution)/shard_map/ppermute | solution.py:13
  543.9 25.5 %collective-permute-start.4 = (bf16[32,16384]{1,0:T(8,128)(2,1)S(1)}, bf16[32,16384]{1,0:T(8,128)(2,1)S(1)}, u32[]{:S(2)}, u32[]{:S(2)}) collective-permute-start(bf16[32,16384]{1,0:T(8,128)(2,1)S(1)} %get-tuple-element.9), channel_id=1, source_target_pairs={{4,0},{8,4},{12,8},{16,12},{20,16},{24,20},{28,24},{32,28},{36,32}... | collective-permute-start | bytes 3145736 | tf_op jit(solution)/shard_map/ppermute | solution.py:13
  621.5 61.5 %copy-start.2 = (bf16[256,32,128]{2,1,0:T(8,128)(2,1)S(1)}, bf16[256,32,128]{2,1,0:T(8,128)(2,1)}, u32[]{:S(2)}) copy-start(bf16[256,32,128]{2,1,0:T(8,128)(2,1)} %gather_fusion.1) | copy-start | bytes 6291460
  624.3 58.7 %collective-permute-start.7 = (f32[32,128,128]{2,0,1:T(8,128)S(1)}, f32[32,128,128]{2,0,1:T(8,128)S(1)}, u32[]{:S(2)}, u32[]{:S(2)}) collective-permute-start(f32[32,128,128]{2,0,1:T(8,128)S(1)} %get-tuple-element.16), channel_id=1, source_target_pairs={{0,8},{4,12},{8,16},{12,20},{16,24},{20,28},{24,32},{28,36},{32,40... | collective-permute-start | bytes 6291464 | tf_op jit(solution)/shard_map/ppermute | solution.py:13
  637.1 45.9 %collective-permute-start.6 = (f32[32,128,128]{2,0,1:T(8,128)S(1)}, f32[32,128,128]{2,0,1:T(8,128)S(1)}, u32[]{:S(2)}, u32[]{:S(2)}) collective-permute-start(f32[32,128,128]{2,0,1:T(8,128)S(1)} %get-tuple-element.15), channel_id=1, source_target_pairs={{0,4},{4,8},{8,12},{12,16},{16,20},{20,24},{24,28},{28,32},{32,36}... | collective-permute-start | bytes 6291464 | tf_op jit(solution)/shard_map/ppermute | solution.py:13
Sparse Core Ops, SparseCore 0:
  159.6 114.9 all-gather.4
  691.5 107.9 all-gather.6
